TPU v7x, 256 devices: a whole 4x4x8 slice. The times are simulated.
256 devices in a mesh: rows: 64 (over x, z, core), grp: 4 (over y).
Axes of the slice: x: 4, y: 4, z: 8, core: 2. Of those that a mesh axis runs over, the one named last changes fastest.
Arguments:
- tile_factor: bfloat16 [512, 128, 128], P(('rows', 'grp')), may hold values from -6 to 6
- coupling: bfloat16 [512, 3, 128, 128], P(('rows', 'grp')), may hold values from -6 to 6
- nbr_list: int32 [512, 4], P('rows'), may hold values from 0 to 511, as said below
- setup_slot: int32 [64, 8], P('rows'), may hold values from 0 to 7, each once within a row
- residual: float32 [256, 65536], P('grp', 'rows'), may hold values from -6 to 6
Outputs:
- factor_rows: float32 [512, 128, 512], P(('rows', 'grp'))
- preconditioned: float32 [256, 65536], P('grp', 'rows')
Inputs may be any that keep to these rules, and one draw needn't show every extreme that they name: `nbr_list`: row i lists 4 distinct block rows: i itself, at some position, and others at distance 1, 3 or 4 from i. `setup_slot`: each slab's row holds every slot once.
All inputs are finite; a program needn't handle non-finite values.
Results may differ from a plain program's by a relative error of at most 0.00065.
Values may be sent and summed in bfloat16 or wider, within the bound.
A program may use at most 64 MiB of HBM per device.

v0:
```python
import functools

import jax
import jax.numpy as jnp
from jax import lax
from jax.experimental import pallas as pl
from jax.experimental.pallas import tpu as pltpu
from jax.sharding import PartitionSpec as P

F32 = jnp.float32
BF = jnp.bfloat16
MESH = pl.DeviceIdType.MESH
B = 128
PAT = 4
NBR = 8
REACH = (-4, -3, -1, 1, 3, 4)
DOUBLINGS = 15


def split(x):
    high = x.astype(BF)
    return high, (x - high.astype(F32)).astype(BF)


def dg(a, b, ca, cb):
    return lax.dot_general(a, b, (((ca,), (cb,)), ((), ())), preferred_element_type=F32)


def mm(a, b, ca=1, cb=0):
    return dg(a[0], b[0], ca, cb) + (dg(a[0], b[1], ca, cb) + dg(a[1], b[0], ca, cb))


def eye():
    shape = (B, B)
    return (lax.broadcasted_iota(jnp.int32, shape, 0) == lax.broadcasted_iota(jnp.int32, shape, 1)).astype(F32)


def inverses(mats):
    unit = eye()
    scales = []
    for mat in mats:
        norm = jnp.max(jnp.sum(jnp.abs(mat), axis=0, keepdims=True), axis=1, keepdims=True)
        scales.append(1.98 / norm)
    start = tuple((unit - mat * scale, unit) for mat, scale in zip(mats, scales))

    def double(_, state):
        new = []
        for power, series in state:
            ph, pl_ = split(power)
            sh, sl = split(series)
            first = jnp.concatenate([ph, sh], axis=1)
            out = dg(jnp.concatenate([ph, pl_], axis=1), jnp.concatenate([first, first], axis=0), 1, 0)
            out = out + dg(ph, jnp.concatenate([pl_, sl], axis=1), 1, 0)
            new.append((out[:, :B], series + out[:, B:]))
        return tuple(new)

    state = lax.fori_loop(0, DOUBLINGS, double, start)
    result = []
    for mat, scale, (_, series) in zip(mats, scales, state):
        guess = series * scale
        gs = split(guess)
        miss = unit - mm(split(mat), gs)
        result.append(guess + mm(gs, split(miss)))
    return result


def sweep(first, last, slabs):
    lane = lax.broadcasted_iota(jnp.int32, (1, B), 1)
    sub = lax.broadcasted_iota(jnp.int32, (8, 1), 0)

    def round_(it, state):
        done = []
        for mat in state:
            mat = list(mat)
            live = [(it <= p).astype(F32) for p in range(15)]
            for s in range(7, -1, -1):
                at = 120 + s
                row = mat[15][s:s + 1, :]
                pivot = row[:, at:at + 1]
                inv = 1.0 / pivot
                scaled = jnp.where(lane == at, 1.0 + inv, row * inv)
                for p in range(16):
                    c = mat[p][:, at:at + 1]
                    if p == 15:
                        if s == 0:
                            continue
                        c = jnp.where(sub < s, c, 0.0)
                    else:
                        c = c * live[p]
                    mat[p] = mat[p] - c * scaled
                final = jnp.where((lane >= 8 * it) & (lane < at), 0.0, jnp.where(lane == at, 1.0, row)) * lax.rsqrt(pivot)
                mat[15] = jnp.where(sub == s, final, mat[15])
            mat = [pltpu.roll(x, 8, 1) for x in mat]
            done.append(tuple([mat[15]] + mat[:15]))
        return tuple(done)

    return lax.fori_loop(first, last, round_, slabs)


def linked(x, y):
    gap = jnp.abs(x - y)
    return (gap == 1) | (gap == 3) | (gap == 4)


def tile_of(gap):
    return jnp.where(gap == 1, 1, jnp.where((gap == 3) | (gap == 4), 2, jnp.where(gap == -3, 1, 0)))


def order(p, i):
    s = jnp.where(p[0] == i, 0, jnp.where(p[1] == i, 1, jnp.where(p[2] == i, 2, 3)))
    pos = [jnp.where(s <= k, k + 1, k) for k in range(3)]
    nb = [jnp.where(s <= k, p[k + 1], p[k]) for k in range(3)]
    mid = jnp.where(linked(nb[1], nb[2]), jnp.where(linked(nb[0], nb[2]), 2, 1), 0)

    def three(v):
        b = jnp.where(mid == 0, v[0], jnp.where(mid == 1, v[1], v[2]))
        return jnp.where(mid == 0, v[1], v[0]), b, jnp.where(mid == 2, v[1], v[2])

    return three(nb), three(pos), s


def kernel(rows, nbr, slot, tf, cp, res, out_f, out_x, near, yall, uall, x3, acc, tsend, trecv,
           own_sem, x_sem, near_send, near_recv, y_send, y_recv, u_send, u_recv, t_sem, xr_sem):
    r = lax.axis_index("rows")
    g = lax.axis_index("grp")
    m = r * 4 + g
    count = rows * 4
    after = lax.rem(m + 1, count)
    before = lax.rem(m + count - 1, count)
    nxt = (after // 4, lax.rem(after, 4))
    prv = (before // 4, lax.rem(before, 4))
    up = (lax.rem(r + 1, rows), g)
    down = (lax.rem(r + rows - 1, rows), g)
    right = (r, lax.rem(g + 1, 4))
    left = (r, lax.rem(g + 3, 4))

    def remote(src, dst, ssem, rsem, dev):
        return pltpu.make_async_remote_copy(
            src_ref=src, dst_ref=dst, send_sem=ssem, recv_sem=rsem, device_id=dev, device_id_type=MESH)

    own = [pltpu.make_async_copy(cp.at[w], near.at[4 + w, pl.ds(0, 3)], own_sem.at[w]) for w in range(2)]
    own += [pltpu.make_async_copy(tf.at[w], near.at[4 + w, 3], own_sem.at[2 + w]) for w in range(2)]
    own += [pltpu.make_async_copy(res.at[:, pl.ds(B * e, B)], x3.at[4 + e], x_sem.at[e]) for e in range(8)]
    for copy in own:
        copy.start()

    barrier = pltpu.get_barrier_semaphore()
    for dev in (nxt, prv, up, down, right, left):
        pl.semaphore_signal(barrier, inc=1, device_id=dev, device_id_type=MESH)
    pl.semaphore_wait(barrier, 6)

    def source(w, t):
        return cp.at[w, t] if t < 3 else tf.at[w]

    sends = []

    def send(src, q, t, dev, lane):
        copy = remote(src, near.at[q, t], near_send.at[lane, t], near_recv.at[q, t], dev)
        copy.start()
        sends.append(copy)

    def arrived(q, t):
        remote(near.at[q, t], near.at[q, t], near_send.at[0, t], near_recv.at[q, t], nxt).wait_recv()

    for t in range(4):
        send(source(0, t), 2, t, nxt, 0)
        send(source(1, t), 7, t, prv, 1)
    for t in range(4):
        send(source(1, t), 3, t, nxt, 2)
        send(source(0, t), 6, t, prv, 3)
    halo = []
    for e in range(4):
        halo.append(remote(res.at[:, pl.ds(B * (4 + e), B)], x3.at[e], xr_sem.at[0, e], xr_sem.at[1, e], up))
        halo.append(remote(res.at[:, pl.ds(B * e, B)], x3.at[12 + e], xr_sem.at[2, e], xr_sem.at[3, e], down))
    for t in range(4):
        arrived(2, t)
        send(near.at[2, t], 0, t, nxt, 4)
        arrived(7, t)
        send(near.at[7, t], 9, t, prv, 5)
    for t in range(4):
        arrived(0, t)
        send(near.at[0, t], 8, t, down, 6)
        arrived(9, t)
        send(near.at[9, t], 1, t, up, 7)
    for copy in halo:
        copy.start()
    for copy in own:
        copy.wait()
    for t in range(4):
        for q in (3, 6, 8, 1):
            arrived(q, t)

    base = 2 * m - 4
    unit = eye()

    def picks(t):
        return order([nbr[t, k] for k in range(PAT)], NBR * r + t)

    def place(j):
        return jnp.clip(j - base, 0, 9)

    def diag(j):
        total = None
        for k in range(4):
            tile = near[place(j), k]
            part = dg(tile, tile, 1, 1)
            total = part if total is None else total + part
        return 2.0 * unit + total * (1.0 / B)

    def off(x, y):
        scale = jnp.where(linked(x, y), 1.0 / B, 0.0).astype(F32)
        return dg(near[place(x), tile_of(y - x)], near[place(y), tile_of(x - y)], 1, 1) * scale

    mine = [2 * g + w for w in range(2)]
    nodes = [picks(t)[0] for t in mine]
    ends = inverses([diag(nodes[w][k]) for w in range(2) for k in (0, 2)])
    held = []
    for w in range(2):
        i = NBR * r + mine[w]
        a, b, c = nodes[w]
        ia, ib, ic = split(off(i, a)), off(i, b), split(off(i, c))
        ab, cb = split(off(a, b)), split(off(c, b))
        inv_a, inv_c = split(ends[2 * w]), split(ends[2 * w + 1])
        za, zc = mm(ia, inv_a), mm(ic, inv_c)
        va, vc = split(mm(inv_a, ab)), split(mm(inv_c, cb))
        schur = diag(b) - mm(ab, va, 0, 0) - mm(cb, vc, 0, 0)
        rest_ib = ib - mm(ia, va) - mm(ic, vc)
        rest_ii = diag(i) - mm(split(za), ia, 1, 1) - mm(split(zc), ic, 1, 1)
        held.append((za, zc, va, vc, schur, rest_ib, rest_ii))
    mids = inverses([h[4] for h in held])
    tops = []
    for w in range(2):
        za, zc, va, vc, _, rest_ib, rest_ii = held[w]
        rs = split(rest_ib)
        yb = mm(rs, split(mids[w]))
        ys = split(yb)
        yall[mine[w], 0] = za - mm(ys, va, 1, 1)
        yall[mine[w], 1] = yb
        yall[mine[w], 2] = zc - mm(ys, vc, 1, 1)
        tops.append(rest_ii - mm(ys, rs, 1, 1))

    def y_copy(t, k, dev, lane):
        return remote(yall.at[t, k], yall.at[t, k], y_send.at[lane, k], y_recv.at[t, k], dev)

    def u_copy(t, dev, lane):
        return remote(uall.at[t], uall.at[t], u_send.at[lane], u_recv.at[t], dev)

    from_left = 2 * lax.rem(g + 3, 4)
    from_right = 2 * lax.rem(g + 1, 4)
    across = 2 * lax.rem(g + 2, 4)
    y_sends = []
    for k in range(3):
        y_sends += [y_copy(mine[0], k, right, 0), y_copy(mine[1], k, left, 1)]
    for k in range(3):
        y_sends += [y_copy(mine[1], k, right, 2), y_copy(mine[0], k, left, 3)]
    for copy in y_sends:
        copy.start()

    slabs = tuple(tuple(top[8 * p:8 * p + 8, :] for p in range(16)) for top in tops)
    for part in range(4):
        slabs = sweep(4 * part, 4 * part + 4, slabs)
        if part < 3:
            y_copy(from_left, part, right, 0).wait_recv()
            copy = y_copy(from_left, part, right, 4)
            copy.start()
            y_sends.append(copy)
            y_copy(from_right + 1, part, left, 0).wait_recv()
            copy = y_copy(from_right + 1, part, left, 5)
            copy.start()
            y_sends.append(copy)
    for w in range(2):
        uall[mine[w]] = jnp.concatenate(slabs[w], axis=0)
    u_sends = [u_copy(mine[0], right, 0), u_copy(mine[1], left, 1), u_copy(mine[1], right, 2), u_copy(mine[0], left, 3)]
    for copy in u_sends:
        copy.start()

    acc[...] = jnp.zeros_like(acc)
    for copy in halo:
        copy.wait()

    def gather(t):
        ids, _, _ = picks(t)
        x = jnp.concatenate([x3[jnp.clip(j - (NBR * r - 4), 0, 15)] for j in ids], axis=1)
        y = jnp.concatenate([yall[t, k] for k in range(3)], axis=1)
        ysp = split(y)
        return x3[4 + t] - mm(split(x), ysp, 1, 1)

    def spread(t, v):
        ids, _, _ = picks(t)
        u = split(uall[t])
        w = mm(split(mm(split(v), u, 1, 1)), u)
        y = jnp.concatenate([yall[t, k] for k in range(3)], axis=1)
        terms = mm(split(w), split(y))
        acc[4 + t] += w
        for gap in REACH:
            part = None
            for k in range(3):
                weight = jnp.where(ids[k] == NBR * r + t + gap, 1.0, 0.0).astype(F32)
                term = terms[:, B * k:B * k + B] * weight
                part = term if part is None else part + term
            acc[4 + t + gap] -= part

    vs = [gather(t) for t in mine]
    u_copy(from_left, right, 0).wait_recv()
    copy = u_copy(from_left, right, 4)
    copy.start()
    u_sends.append(copy)
    u_copy(from_right + 1, left, 0).wait_recv()
    copy = u_copy(from_right + 1, left, 5)
    copy.start()
    u_sends.append(copy)
    for t, v in zip(mine, vs):
        spread(t, v)
    others = [from_left, from_right + 1, from_left + 1, from_right]
    for t in others[2:]:
        for k in range(3):
            y_copy(t, k, right, 0).wait_recv()
        u_copy(t, right, 0).wait_recv()
    for t in others:
        spread(t, gather(t))
    for t in (across, across + 1):
        for k in range(3):
            y_copy(t, k, right, 0).wait_recv()
    vs = [gather(t) for t in (across, across + 1)]
    for t, v in zip((across, across + 1), vs):
        u_copy(t, right, 0).wait_recv()
        spread(t, v)

    for e in range(4):
        tsend[0, e] = acc[e].astype(BF)
        tsend[1, e] = acc[12 + e].astype(BF)
    swaps = [remote(tsend.at[0], trecv.at[0], t_sem.at[0], t_sem.at[1], down),
             remote(tsend.at[1], trecv.at[1], t_sem.at[2], t_sem.at[3], up)]
    for copy in swaps:
        copy.start()

    for w in range(2):
        t = 0
        for k in range(NBR):
            t = t + jnp.where(slot[0, k] == 2 * g + w, k, 0)
        t = jnp.minimum(t, NBR - 1)
        _, pos, s = picks(t)
        u = uall[t]
        us = split(u)
        for a in range(PAT):
            k = jnp.where(pos[1] == a, 1, jnp.where(pos[2] == a, 2, 0))
            self_ = (s == a).astype(F32)
            out_f[w, :, B * a:B * a + B] = u * self_ - mm(us, split(yall[t, k])) * (1.0 - self_)

    for copy in swaps:
        copy.wait()
    for e in range(4):
        out_x[:, B * e:B * e + B] = acc[4 + e] + trecv[1, e].astype(F32)
        out_x[:, B * (4 + e):B * (4 + e) + B] = acc[8 + e] + trecv[0, e].astype(F32)
    for copy in sends + y_sends + u_sends:
        copy.wait_send()


def solution(mesh):
    rows = mesh.shape["rows"]
    smem = pl.BlockSpec(memory_space=pltpu.SMEM)
    raw = pl.BlockSpec(memory_space=pl.ANY)
    whole = pl.BlockSpec(memory_space=pltpu.VMEM)

    def local(tile_factor, coupling, nbr_list, setup_slot, residual):
        columns = residual.shape[0]
        dma = pltpu.SemaphoreType.DMA
        factor, result = pl.pallas_call(
            functools.partial(kernel, rows),
            out_shape=(
                jax.ShapeDtypeStruct((2, B, PAT * B), F32),
                jax.ShapeDtypeStruct((columns, NBR * B), F32),
            ),
            in_specs=[smem, smem, raw, raw, raw],
            out_specs=(whole, whole),
            scratch_shapes=[
                pltpu.VMEM((10, 4, B, B), BF),
                pltpu.VMEM((NBR, 3, B, B), F32),
                pltpu.VMEM((NBR, B, B), F32),
                pltpu.VMEM((16, columns, B), F32),
                pltpu.VMEM((16, columns, B), F32),
                pltpu.VMEM((2, 4, columns, B), BF),
                pltpu.VMEM((2, 4, columns, B), BF),
                dma((4,)), dma((8,)), dma((8, 4)), dma((10, 4)), dma((6, 3)), dma((NBR, 3)),
                dma((6,)), dma((NBR,)), dma((4,)), dma((4, 4)),
            ],
            compiler_params=pltpu.CompilerParams(
                collective_id=0, has_side_effects=True, vmem_limit_bytes=48 * 1024 * 1024
            ),
        )(nbr_list, setup_slot, tile_factor, coupling, residual)
        return factor, result

    return jax.shard_map(
        local,
        mesh=mesh,
        in_specs=(
            P(("rows", "grp"), None, None),
            P(("rows", "grp"), None, None, None),
            P("rows", None),
            P("rows", None),
            P("grp", "rows"),
        ),
        out_specs=(P(("rows", "grp"), None, None), P("grp", "rows")),
        check_vma=False,
    )
```

profile of v0, /device:TPU:16, one launch (start us, length us, event | category | flops | bytes accessed | tf_op | source)
XLA Modules:
  0.0 72.2 jit_solution(16874009679644251879)
XLA Ops:
  0.6 0.0 copy-start.3
  0.6 0.8 %copy.7.nbr = s32[8,4]{1,0:T(8,128)S(1)} copy(s32[8,4]{0,1:T(4,128)} %param.7) | data formatting | bytes 256 | tf_op args[2]
  1.4 0.0 copy-done.3
  1.4 0.0 copy-start
  1.4 0.9 %copy-done = f32[64,1024]{1,0:T(8,128)S(1)} copy-done((f32[64,1024]{1,0:T(8,128)S(1)}, f32[64,1024]{1,0:T(8,128)}, u32[]{:S(2)}) %copy-start) | copy-done | bytes 262168
  2.4 0.0 copy-start.1
  2.4 0.9 %copy-done.1 = bf16[2,3,128,128]{3,2,1,0:T(8,128)(2,1)S(1)} copy-done((bf16[2,3,128,128]{3,2,1,0:T(8,128)(2,1)S(1)}, bf16[2,3,128,128]{3,2,1,0:T(8,128)(2,1)}, u32[]{:S(2)}) %copy-start.1) | copy-done | bytes 196632
  3.3 0.0 copy-start.2
  3.3 0.8 %copy-done.2 = bf16[2,128,128]{2,1,0:T(8,128)(2,1)S(1)} copy-done((bf16[2,128,128]{2,1,0:T(8,128)(2,1)S(1)}, bf16[2,128,128]{2,1,0:T(8,128)(2,1)}, u32[]{:S(2)}) %copy-start.2) | copy-done | bytes 65560
  4.1 66.5 %shard_map.68 = (f32[2,128,512]{2,1,0:T(8,128)S(1)}, f32[64,1024]{1,0:T(8,128)S(1)}) custom-call(s32[8,4]{1,0:T(8,128)S(1)} %copy.7.nbr, s32[1,8]{1,0:T(1,128)S(1)} %copy-done.3, bf16[2,128,128]{2,1,0:T(8,128)(2,1)S(1)} %copy-done.2, bf16[2,3,128,128]{3,2,1,0:T(8,128)(2,1)S(1)} %copy-done.1, f32[64,1024]{1,0:T(8,128)S(1)} %copy-done), custom_call_target="tpu_custom_call" | custom-call | tf_op jit(solution)/shard_map/pallas_call | solution.py:368
  70.7 0.8 %copy.10 = f32[2,128,512]{2,1,0:T(8,128)} copy(f32[2,128,512]{2,1,0:T(8,128)S(1)} %get-tuple-element.4) | data formatting | bytes 1048576
  71.5 0.7 copy.11
Async XLA Ops:
  0.6 0.8 %copy-start.3 = (s32[1,8]{1,0:T(1,128)S(1)}, s32[1,8]{1,0:T(1,128)}, u32[]{:S(2)}) copy-start(s32[1,8]{1,0:T(1,128)} %slot.1) | copy-start | bytes 100
  1.4 1.0 %copy-start = (f32[64,1024]{1,0:T(8,128)S(1)}, f32[64,1024]{1,0:T(8,128)}, u32[]{:S(2)}) copy-start(f32[64,1024]{1,0:T(8,128)} %res.1) | copy-start | bytes 786436
  2.4 0.9 %copy-start.1 = (bf16[2,3,128,128]{3,2,1,0:T(8,128)(2,1)S(1)}, bf16[2,3,128,128]{3,2,1,0:T(8,128)(2,1)}, u32[]{:S(2)}) copy-start(bf16[2,3,128,128]{3,2,1,0:T(8,128)(2,1)} %cp.1) | copy-start | bytes 589828
  3.3 0.8 %copy-start.2 = (bf16[2,128,128]{2,1,0:T(8,128)(2,1)S(1)}, bf16[2,128,128]{2,1,0:T(8,128)(2,1)}, u32[]{:S(2)}) copy-start(bf16[2,128,128]{2,1,0:T(8,128)(2,1)} %tf.1) | copy-start | bytes 196612
where the time goes:
time: 72.4 us; the launch traced here: 72.2 us
  Pallas kernels  66.5 us (92%)
  local copies, waits for them, and re-layouts  4.98 us (7%)
    pallas_call x1, Pallas kernels, local(): pl.pallas_call(functools.partial(kernel, rows), out_shape=(jax.ShapeDtype...  66.5 us
    unnamed x11, local copies, waits for them, and re-layouts  4.98 us

commit v1 on v0

--- a/solution.py
+++ b/solution.py
@@ -125,14 +125,23 @@
     g = lax.axis_index("grp")
     m = r * 4 + g
     count = rows * 4
-    after = lax.rem(m + 1, count)
-    before = lax.rem(m + count - 1, count)
+    has_nxt, has_prv = m < count - 1, m > 0
+    has_up, has_down = r < rows - 1, r > 0
+    inner = has_nxt & has_prv
+    after = jnp.minimum(m + 1, count - 1)
+    before = jnp.maximum(m - 1, 0)
     nxt = (after // 4, lax.rem(after, 4))
     prv = (before // 4, lax.rem(before, 4))
-    up = (lax.rem(r + 1, rows), g)
-    down = (lax.rem(r + rows - 1, rows), g)
+    up = (jnp.minimum(r + 1, rows - 1), g)
+    down = (jnp.maximum(r - 1, 0), g)
     right = (r, lax.rem(g + 1, 4))
     left = (r, lax.rem(g + 3, 4))
+
+    def when(there, act):
+        if there is None:
+            act()
+        else:
+            pl.when(there)(act)
 
     def remote(src, dst, ssem, rsem, dev):
         return pltpu.make_async_remote_copy(
@@ -144,57 +153,72 @@
     for copy in own:
         copy.start()
 
+    def blank(side):
+        trecv[side] = jnp.zeros_like(trecv[side])
+
+    when(r == rows - 1, lambda: blank(0))
+    when(r == 0, lambda: blank(1))
     barrier = pltpu.get_barrier_semaphore()
-    for dev in (nxt, prv, up, down, right, left):
-        pl.semaphore_signal(barrier, inc=1, device_id=dev, device_id_type=MESH)
-    pl.semaphore_wait(barrier, 6)
+    for there, dev in ((has_nxt, nxt), (has_prv, prv), (has_up, up), (has_down, down), (None, right), (None, left)):
+        when(there, lambda: pl.semaphore_signal(barrier, inc=1, device_id=dev, device_id_type=MESH))
+    partners = 2
+    for there in (has_nxt, has_prv, has_up, has_down):
+        partners = partners + there.astype(jnp.int32)
+    pl.semaphore_wait(barrier, partners)
 
     def source(w, t):
         return cp.at[w, t] if t < 3 else tf.at[w]
 
     sends = []
 
-    def send(src, q, t, dev, lane):
+    def send(there, src, q, t, dev, lane):
         copy = remote(src, near.at[q, t], near_send.at[lane, t], near_recv.at[q, t], dev)
-        copy.start()
-        sends.append(copy)
-
-    def arrived(q, t):
-        remote(near.at[q, t], near.at[q, t], near_send.at[0, t], near_recv.at[q, t], nxt).wait_recv()
-
-    for t in range(4):
-        send(source(0, t), 2, t, nxt, 0)
-        send(source(1, t), 7, t, prv, 1)
-    for t in range(4):
-        send(source(1, t), 3, t, nxt, 2)
-        send(source(0, t), 6, t, prv, 3)
+        when(there, copy.start)
+        sends.append((there, copy))
+
+    def arrived(there, q, t):
+        when(there, remote(near.at[q, t], near.at[q, t], near_send.at[0, t], near_recv.at[q, t], nxt).wait_recv)
+
+    for t in range(4):
+        send(has_nxt, source(0, t), 2, t, nxt, 0)
+        send(has_prv, source(1, t), 7, t, prv, 1)
+    for t in range(4):
+        send(has_nxt, source(1, t), 3, t, nxt, 2)
+        send(has_prv, source(0, t), 6, t, prv, 3)
     halo = []
     for e in range(4):
-        halo.append(remote(res.at[:, pl.ds(B * (4 + e), B)], x3.at[e], xr_sem.at[0, e], xr_sem.at[1, e], up))
-        halo.append(remote(res.at[:, pl.ds(B * e, B)], x3.at[12 + e], xr_sem.at[2, e], xr_sem.at[3, e], down))
-    for t in range(4):
-        arrived(2, t)
-        send(near.at[2, t], 0, t, nxt, 4)
-        arrived(7, t)
-        send(near.at[7, t], 9, t, prv, 5)
-    for t in range(4):
-        arrived(0, t)
-        send(near.at[0, t], 8, t, down, 6)
-        arrived(9, t)
-        send(near.at[9, t], 1, t, up, 7)
-    for copy in halo:
-        copy.start()
+        halo.append((has_up, has_down, remote(res.at[:, pl.ds(B * (4 + e), B)], x3.at[e], xr_sem.at[0, e], xr_sem.at[1, e], up)))
+        halo.append((has_down, has_up, remote(res.at[:, pl.ds(B * e, B)], x3.at[12 + e], xr_sem.at[2, e], xr_sem.at[3, e], down)))
+    middle = (g == 1) | (g == 2)
+    first_slab, last_slab = middle & (r == 0), middle & (r == rows - 1)
+    for t in range(4):
+        arrived(has_prv, 2, t)
+        send(inner, near.at[2, t], 0, t, nxt, 4)
+        arrived(has_nxt, 7, t)
+        send(inner, near.at[7, t], 9, t, prv, 5)
+    for t in range(4):
+        arrived(has_prv, 3, t)
+        send(first_slab, near.at[3, t], 1, t, nxt, 8)
+        arrived(has_nxt, 6, t)
+        send(last_slab, near.at[6, t], 8, t, prv, 9)
+    for t in range(4):
+        arrived(m > 1, 0, t)
+        send(has_down, near.at[0, t], 8, t, down, 6)
+        arrived(m < count - 2, 9, t)
+        send(has_up, near.at[9, t], 1, t, up, 7)
+    for there, _, copy in halo:
+        when(there, copy.start)
     for copy in own:
         copy.wait()
     for t in range(4):
-        for q in (3, 6, 8, 1):
-            arrived(q, t)
+        arrived(m < count - 2, 8, t)
+        arrived(m > 1, 1, t)
 
     base = 2 * m - 4
     unit = eye()
 
     def picks(t):
-        return order([nbr[t, k] for k in range(PAT)], NBR * r + t)
+        return order([nbr[k, t] for k in range(PAT)], NBR * r + t)
 
     def place(j):
         return jnp.clip(j - base, 0, 9)
@@ -275,8 +299,9 @@
         copy.start()
 
     acc[...] = jnp.zeros_like(acc)
-    for copy in halo:
-        copy.wait()
+    for there, back, copy in halo:
+        when(there, copy.wait_send)
+        when(back, copy.wait_recv)
 
     def gather(t):
         ids, _, _ = picks(t)
@@ -329,10 +354,10 @@
     for e in range(4):
         tsend[0, e] = acc[e].astype(BF)
         tsend[1, e] = acc[12 + e].astype(BF)
-    swaps = [remote(tsend.at[0], trecv.at[0], t_sem.at[0], t_sem.at[1], down),
-             remote(tsend.at[1], trecv.at[1], t_sem.at[2], t_sem.at[3], up)]
-    for copy in swaps:
-        copy.start()
+    swaps = [(has_down, has_up, remote(tsend.at[0], trecv.at[0], t_sem.at[0], t_sem.at[1], down)),
+             (has_up, has_down, remote(tsend.at[1], trecv.at[1], t_sem.at[2], t_sem.at[3], up))]
+    for there, _, copy in swaps:
+        when(there, copy.start)
 
     for w in range(2):
         t = 0
@@ -347,19 +372,22 @@
             self_ = (s == a).astype(F32)
             out_f[w, :, B * a:B * a + B] = u * self_ - mm(us, split(yall[t, k])) * (1.0 - self_)
 
-    for copy in swaps:
-        copy.wait()
+    for there, back, copy in swaps:
+        when(there, copy.wait_send)
+        when(back, copy.wait_recv)
     for e in range(4):
         out_x[:, B * e:B * e + B] = acc[4 + e] + trecv[1, e].astype(F32)
         out_x[:, B * (4 + e):B * (4 + e) + B] = acc[8 + e] + trecv[0, e].astype(F32)
-    for copy in sends + y_sends + u_sends:
+    for there, copy in sends:
+        when(there, copy.wait_send)
+    for copy in y_sends + u_sends:
         copy.wait_send()
 
 
 def solution(mesh):
     rows = mesh.shape["rows"]
     smem = pl.BlockSpec(memory_space=pltpu.SMEM)
-    raw = pl.BlockSpec(memory_space=pl.ANY)
+    raw = pl.BlockSpec(memory_space=pltpu.HBM)
     whole = pl.BlockSpec(memory_space=pltpu.VMEM)
 
     def local(tile_factor, coupling, nbr_list, setup_slot, residual):
@@ -381,13 +409,13 @@
                 pltpu.VMEM((16, columns, B), F32),
                 pltpu.VMEM((2, 4, columns, B), BF),
                 pltpu.VMEM((2, 4, columns, B), BF),
-                dma((4,)), dma((8,)), dma((8, 4)), dma((10, 4)), dma((6, 3)), dma((NBR, 3)),
+                dma((4,)), dma((8,)), dma((10, 4)), dma((10, 4)), dma((6, 3)), dma((NBR, 3)),
                 dma((6,)), dma((NBR,)), dma((4,)), dma((4, 4)),
             ],
             compiler_params=pltpu.CompilerParams(
-                collective_id=0, has_side_effects=True, vmem_limit_bytes=48 * 1024 * 1024
+                collective_id=0, has_side_effects=True, vmem_limit_bytes=67043328
             ),
-        )(nbr_list, setup_slot, tile_factor, coupling, residual)
+        )(nbr_list.T, setup_slot, tile_factor, coupling, residual)
         return factor, result
 
     return jax.shard_map(

time: 72.4 us -> 67.7 us (0.935)
  the two profiles are of different devices: /device:TPU:16 before, /device:TPU:6 now
where the time goes in v1:
time: 67.7 us; the launch traced here: 67.6 us
  Pallas kernels  64.3 us (95%)
  local copies, waits for them, and re-layouts  2.62 us (4%)
    pallas_call x1, Pallas kernels, local(): pl.pallas_call(functools.partial(kernel, rows), out_shape=(jax.ShapeDtype...  64.3 us
    unnamed x4, local copies, waits for them, and re-layouts  2.62 us

profile of v1, /device:TPU:6, one launch (start us, length us, event | category | flops | bytes accessed | tf_op | source)
XLA Modules:
  0.0 67.6 jit_solution(4418746872378823158)
XLA Ops:
  0.6 64.3 %shard_map.68 = (f32[2,128,512]{2,1,0:T(8,128)}, f32[64,1024]{1,0:T(8,128)}) custom-call(s32[4,8]{1,0:T(4,128)} %bitcast.1, s32[1,8]{1,0:T(1,128)} %slot.1, bf16[2,128,128]{2,1,0:T(8,128)(2,1)} %tf.1, bf16[2,3,128,128]{3,2,1,0:T(8,128)(2,1)} %cp.1, f32[64,1024]{1,0:T(8,128)} %res.1), custom_call_target="tpu_custom_call" | custom-call | tf_op jit(solution)/shard_map/pallas_call | solution.py:396
  64.9 0.0 copy-start
  65.0 1.9 %copy.9 = f32[2,128,512]{2,1,0:T(8,128)} copy(f32[2,128,512]{2,1,0:T(8,128)} %get-tuple-element.4) | data formatting | bytes 1048576
  66.9 0.0 copy-done
  66.9 0.7 %copy.10 = f32[64,1024]{1,0:T(8,128)} copy(f32[64,1024]{1,0:T(8,128)S(1)} %copy-done) | data formatting | bytes 524288
Async XLA Ops:
  64.9 1.9 %copy-start = (f32[64,1024]{1,0:T(8,128)S(1)}, f32[64,1024]{1,0:T(8,128)}, u32[]{:S(2)}) copy-start(f32[64,1024]{1,0:T(8,128)} %get-tuple-element.5) | copy-start | bytes 786436

commit v2 on v1

--- a/solution.py
+++ b/solution.py
@@ -14,7 +14,8 @@
 PAT = 4
 NBR = 8
 REACH = (-4, -3, -1, 1, 3, 4)
-DOUBLINGS = 15
+DOUBLINGS = 9
+HALF = 64
 
 
 def split(x):
@@ -30,41 +31,47 @@
     return dg(a[0], b[0], ca, cb) + (dg(a[0], b[1], ca, cb) + dg(a[1], b[0], ca, cb))
 
 
-def eye():
-    shape = (B, B)
+def eye(n=B):
+    shape = (n, n)
     return (lax.broadcasted_iota(jnp.int32, shape, 0) == lax.broadcasted_iota(jnp.int32, shape, 1)).astype(F32)
 
 
 def inverses(mats):
-    unit = eye()
-    scales = []
+    size = mats[0].shape[0]
+    unit = eye(size)
+    start = []
     for mat in mats:
         norm = jnp.max(jnp.sum(jnp.abs(mat), axis=0, keepdims=True), axis=1, keepdims=True)
-        scales.append(1.98 / norm)
-    start = tuple((unit - mat * scale, unit) for mat, scale in zip(mats, scales))
+        scale = 2.0 / (2.0 + norm)
+        start.append((unit - mat * scale, unit * scale, 2.0 * scale))
 
     def double(_, state):
         new = []
-        for power, series in state:
+        for power, series, low in state:
             ph, pl_ = split(power)
             sh, sl = split(series)
-            first = jnp.concatenate([ph, sh], axis=1)
-            out = dg(jnp.concatenate([ph, pl_], axis=1), jnp.concatenate([first, first], axis=0), 1, 0)
-            out = out + dg(ph, jnp.concatenate([pl_, sl], axis=1), 1, 0)
-            new.append((out[:, :B], series + out[:, B:]))
+            gain = low * (2.0 - low)
+            s = 2.0 / (1.0 + gain)
+            if size == B:
+                first = jnp.concatenate([ph, sh], axis=1)
+                out = dg(jnp.concatenate([ph, pl_], axis=1), jnp.concatenate([first, first], axis=0), 1, 0)
+                out = out + dg(ph, jnp.concatenate([pl_, sl], axis=1), 1, 0)
+                square, step = out[:, :B], out[:, B:]
+            else:
+                square, step = mm((ph, pl_), (ph, pl_)), mm((ph, pl_), (sh, sl))
+            new.append((square * s + unit * (1.0 - s), (series + step) * s, gain * s))
         return tuple(new)
 
-    state = lax.fori_loop(0, DOUBLINGS, double, start)
+    state = lax.fori_loop(0, DOUBLINGS, double, tuple(start))
     result = []
-    for mat, scale, (_, series) in zip(mats, scales, state):
-        guess = series * scale
+    for mat, (_, guess, _) in zip(mats, state):
         gs = split(guess)
         miss = unit - mm(split(mat), gs)
         result.append(guess + mm(gs, split(miss)))
     return result
 
 
-def sweep(first, last, slabs):
+def sweep(mats):
     lane = lax.broadcasted_iota(jnp.int32, (1, B), 1)
     sub = lax.broadcasted_iota(jnp.int32, (8, 1), 0)
 
@@ -72,16 +79,16 @@
         done = []
         for mat in state:
             mat = list(mat)
-            live = [(it <= p).astype(F32) for p in range(15)]
+            live = [(it <= p).astype(F32) for p in range(7)]
             for s in range(7, -1, -1):
                 at = 120 + s
-                row = mat[15][s:s + 1, :]
+                row = mat[7][s:s + 1, :]
                 pivot = row[:, at:at + 1]
                 inv = 1.0 / pivot
                 scaled = jnp.where(lane == at, 1.0 + inv, row * inv)
-                for p in range(16):
+                for p in range(8):
                     c = mat[p][:, at:at + 1]
-                    if p == 15:
+                    if p == 7:
                         if s == 0:
                             continue
                         c = jnp.where(sub < s, c, 0.0)
@@ -89,12 +96,13 @@
                         c = c * live[p]
                     mat[p] = mat[p] - c * scaled
                 final = jnp.where((lane >= 8 * it) & (lane < at), 0.0, jnp.where(lane == at, 1.0, row)) * lax.rsqrt(pivot)
-                mat[15] = jnp.where(sub == s, final, mat[15])
+                mat[7] = jnp.where(sub == s, final, mat[7])
             mat = [pltpu.roll(x, 8, 1) for x in mat]
-            done.append(tuple([mat[15]] + mat[:15]))
+            done.append(tuple([mat[7]] + mat[:7]))
         return tuple(done)
 
-    return lax.fori_loop(first, last, round_, slabs)
+    slabs = lax.fori_loop(0, 8, round_, tuple(tuple(x[8 * p:8 * p + 8, :] for p in range(8)) for x in mats))
+    return [jnp.concatenate(x, axis=0) for x in slabs]
 
 
 def linked(x, y):
@@ -189,6 +197,10 @@
     for e in range(4):
         halo.append((has_up, has_down, remote(res.at[:, pl.ds(B * (4 + e), B)], x3.at[e], xr_sem.at[0, e], xr_sem.at[1, e], up)))
         halo.append((has_down, has_up, remote(res.at[:, pl.ds(B * e, B)], x3.at[12 + e], xr_sem.at[2, e], xr_sem.at[3, e], down)))
+    for there, _, copy in halo:
+        when(there, copy.start)
+    for copy in own:
+        copy.wait()
     middle = (g == 1) | (g == 2)
     first_slab, last_slab = middle & (r == 0), middle & (r == rows - 1)
     for t in range(4):
@@ -206,10 +218,6 @@
         send(has_down, near.at[0, t], 8, t, down, 6)
         arrived(m < count - 2, 9, t)
         send(has_up, near.at[9, t], 1, t, up, 7)
-    for there, _, copy in halo:
-        when(there, copy.start)
-    for copy in own:
-        copy.wait()
     for t in range(4):
         arrived(m < count - 2, 8, t)
         arrived(m > 1, 1, t)
@@ -258,9 +266,8 @@
         rs = split(rest_ib)
         yb = mm(rs, split(mids[w]))
         ys = split(yb)
-        yall[mine[w], 0] = za - mm(ys, va, 1, 1)
-        yall[mine[w], 1] = yb
-        yall[mine[w], 2] = zc - mm(ys, vc, 1, 1)
+        for k, y in enumerate((za - mm(ys, va, 1, 1), None, zc - mm(ys, vc, 1, 1))):
+            yall[mine[w], k, 0], yall[mine[w], k, 1] = ys if y is None else split(y)
         tops.append(rest_ii - mm(ys, rs, 1, 1))
 
     def y_copy(t, k, dev, lane):
@@ -280,20 +287,34 @@
     for copy in y_sends:
         copy.start()
 
-    slabs = tuple(tuple(top[8 * p:8 * p + 8, :] for p in range(16)) for top in tops)
-    for part in range(4):
-        slabs = sweep(4 * part, 4 * part + 4, slabs)
-        if part < 3:
-            y_copy(from_left, part, right, 0).wait_recv()
-            copy = y_copy(from_left, part, right, 4)
-            copy.start()
-            y_sends.append(copy)
-            y_copy(from_right + 1, part, left, 0).wait_recv()
-            copy = y_copy(from_right + 1, part, left, 5)
-            copy.start()
-            y_sends.append(copy)
+    upper = lax.broadcasted_iota(jnp.int32, (1, B), 1) >= HALF
+    turned = [pltpu.roll(top, HALF, 1) for top in tops]
+    corners = inverses([x[HALF:, :HALF] for x in turned])
+    work, crosses = [], []
+    for top, x, corner in zip(tops, turned, corners):
+        cross = split(x[:HALF, :HALF])
+        cross_s = mm(cross, split(corner))
+        crosses.append(cross_s)
+        rest = top[:HALF, :HALF] - mm(split(cross_s), cross, 1, 1)
+        blank_half = jnp.zeros((HALF, HALF), F32)
+        work.append(jnp.concatenate([blank_half, rest], axis=1))
+        work.append(jnp.where(upper, top[HALF:, :], 0.0))
+    swept = sweep(work)
     for w in range(2):
-        uall[mine[w]] = jnp.concatenate(slabs[w], axis=0)
+        head, foot = swept[2 * w][:, :HALF], swept[2 * w + 1]
+        edge = mm(split(head), split(crosses[w]))
+        uall[mine[w], 0:HALF, :] = jnp.concatenate([head, -edge], axis=1)
+        uall[mine[w], HALF:HALF + HALF // 2, :] = jnp.concatenate(
+            [foot[:HALF // 2, :HALF], foot[HALF // 2:, :HALF]], axis=1)
+    for part in range(3):
+        y_copy(from_left, part, right, 0).wait_recv()
+        copy = y_copy(from_left, part, right, 4)
+        copy.start()
+        y_sends.append(copy)
+        y_copy(from_right + 1, part, left, 0).wait_recv()
+        copy = y_copy(from_right + 1, part, left, 5)
+        copy.start()
+        y_sends.append(copy)
     u_sends = [u_copy(mine[0], right, 0), u_copy(mine[1], left, 1), u_copy(mine[1], right, 2), u_copy(mine[0], left, 3)]
     for copy in u_sends:
         copy.start()
@@ -303,29 +324,39 @@
         when(there, copy.wait_send)
         when(back, copy.wait_recv)
 
-    def gather(t):
-        ids, _, _ = picks(t)
-        x = jnp.concatenate([x3[jnp.clip(j - (NBR * r - 4), 0, 15)] for j in ids], axis=1)
-        y = jnp.concatenate([yall[t, k] for k in range(3)], axis=1)
-        ysp = split(y)
-        return x3[4 + t] - mm(split(x), ysp, 1, 1)
-
-    def spread(t, v):
-        ids, _, _ = picks(t)
-        u = split(uall[t])
-        w = mm(split(mm(split(v), u, 1, 1)), u)
-        y = jnp.concatenate([yall[t, k] for k in range(3)], axis=1)
-        terms = mm(split(w), split(y))
-        acc[4 + t] += w
-        for gap in REACH:
-            part = None
-            for k in range(3):
-                weight = jnp.where(ids[k] == NBR * r + t + gap, 1.0, 0.0).astype(F32)
-                term = terms[:, B * k:B * k + B] * weight
-                part = term if part is None else part + term
-            acc[4 + t + gap] -= part
-
-    vs = [gather(t) for t in mine]
+    def y_of(t):
+        return tuple(jnp.concatenate([yall[t, k, part] for k in range(3)], axis=1) for part in range(2))
+
+    def gather(ts):
+        seen = []
+        for t in ts:
+            ids, _, _ = picks(t)
+            x = jnp.concatenate([x3[jnp.clip(j - (NBR * r - 4), 0, 15)] for j in ids], axis=1)
+            seen.append((split(x), y_of(t), x3[4 + t]))
+        return [own_x - mm(x, y, 1, 1) for x, y, own_x in seen]
+
+    def factor(t):
+        low = uall[t, HALF:HALF + HALF // 2, :]
+        low = jnp.concatenate([pltpu.roll(low, HALF, 1), low], axis=0)
+        return jnp.concatenate([uall[t, 0:HALF, :], jnp.where(upper, low, 0.0)], axis=0)
+
+    def spread(ts, vs):
+        us = [split(factor(t)) for t in ts]
+        ws = [split(mm(split(v), u, 1, 1)) for v, u in zip(vs, us)]
+        ws = [mm(w, u) for w, u in zip(ws, us)]
+        terms = [mm(split(w), y_of(t)) for w, t in zip(ws, ts)]
+        for t, w, term in zip(ts, ws, terms):
+            ids, _, _ = picks(t)
+            acc[4 + t] += w
+            for gap in REACH:
+                part = None
+                for k in range(3):
+                    weight = jnp.where(ids[k] == NBR * r + t + gap, 1.0, 0.0).astype(F32)
+                    piece = term[:, B * k:B * k + B] * weight
+                    part = piece if part is None else part + piece
+                acc[4 + t + gap] -= part
+
+    vs = gather(mine)
     u_copy(from_left, right, 0).wait_recv()
     copy = u_copy(from_left, right, 4)
     copy.start()
@@ -334,22 +365,21 @@
     copy = u_copy(from_right + 1, left, 5)
     copy.start()
     u_sends.append(copy)
-    for t, v in zip(mine, vs):
-        spread(t, v)
+    spread(mine, vs)
     others = [from_left, from_right + 1, from_left + 1, from_right]
     for t in others[2:]:
         for k in range(3):
             y_copy(t, k, right, 0).wait_recv()
         u_copy(t, right, 0).wait_recv()
-    for t in others:
-        spread(t, gather(t))
-    for t in (across, across + 1):
+    spread(others, gather(others))
+    last = [across, across + 1]
+    for t in last:
         for k in range(3):
             y_copy(t, k, right, 0).wait_recv()
-    vs = [gather(t) for t in (across, across + 1)]
-    for t, v in zip((across, across + 1), vs):
+    vs = gather(last)
+    for t in last:
         u_copy(t, right, 0).wait_recv()
-        spread(t, v)
+    spread(last, vs)
 
     for e in range(4):
         tsend[0, e] = acc[e].astype(BF)
@@ -365,12 +395,12 @@
             t = t + jnp.where(slot[0, k] == 2 * g + w, k, 0)
         t = jnp.minimum(t, NBR - 1)
         _, pos, s = picks(t)
-        u = uall[t]
+        u = factor(t)
         us = split(u)
         for a in range(PAT):
             k = jnp.where(pos[1] == a, 1, jnp.where(pos[2] == a, 2, 0))
             self_ = (s == a).astype(F32)
-            out_f[w, :, B * a:B * a + B] = u * self_ - mm(us, split(yall[t, k])) * (1.0 - self_)
+            out_f[w, :, B * a:B * a + B] = u * self_ - mm(us, (yall[t, k, 0], yall[t, k, 1])) * (1.0 - self_)
 
     for there, back, copy in swaps:
         when(there, copy.wait_send)
@@ -403,8 +433,8 @@
             out_specs=(whole, whole),
             scratch_shapes=[
                 pltpu.VMEM((10, 4, B, B), BF),
-                pltpu.VMEM((NBR, 3, B, B), F32),
-                pltpu.VMEM((NBR, B, B), F32),
+                pltpu.VMEM((NBR, 3, 2, B, B), BF),
+                pltpu.VMEM((NBR, HALF + HALF // 2, B), F32),
                 pltpu.VMEM((16, columns, B), F32),
                 pltpu.VMEM((16, columns, B), F32),
                 pltpu.VMEM((2, 4, columns, B), BF),

time: 67.7 us -> 61.3 us (0.905)
  Pallas kernels: 64.3 us -> 57.9 us
    pallas_call x1, Pallas kernels: 64.3 us -> 57.9 us  [local(): pl.pallas_call(functools.partial(kernel, rows), out_shape=(jax.ShapeDtype...]
where the time goes in v2:
time: 61.3 us; the launch traced here: 61.2 us
  Pallas kernels  57.9 us (94%)
  local copies, waits for them, and re-layouts  2.62 us (4%)
  between operations  0.65 us (1%)
    pallas_call x1, Pallas kernels, local(): pl.pallas_call(functools.partial(kernel, rows), out_shape=(jax.ShapeDtype...  57.9 us
    unnamed x4, local copies, waits for them, and re-layouts  2.62 us

profile of v2, /device:TPU:6, one launch (start us, length us, event | category | flops | bytes accessed | tf_op | source)
XLA Modules:
  0.0 61.2 jit_solution(15184546801496626120)
XLA Ops:
  0.6 57.9 %shard_map.68 = (f32[2,128,512]{2,1,0:T(8,128)}, f32[64,1024]{1,0:T(8,128)}) custom-call(s32[4,8]{1,0:T(4,128)} %bitcast.1, s32[1,8]{1,0:T(1,128)} %slot.1, bf16[2,128,128]{2,1,0:T(8,128)(2,1)} %tf.1, bf16[2,3,128,128]{3,2,1,0:T(8,128)(2,1)} %cp.1, f32[64,1024]{1,0:T(8,128)} %res.1), custom_call_target="tpu_custom_call" | custom-call | tf_op jit(solution)/shard_map/pallas_call | solution.py:426
  58.6 0.0 copy-start
  58.6 1.9 %copy.9 = f32[2,128,512]{2,1,0:T(8,128)} copy(f32[2,128,512]{2,1,0:T(8,128)} %get-tuple-element.4) | data formatting | bytes 1048576
  60.5 0.0 copy-done
  60.5 0.7 %copy.10 = f32[64,1024]{1,0:T(8,128)} copy(f32[64,1024]{1,0:T(8,128)S(1)} %copy-done) | data formatting | bytes 524288
Async XLA Ops:
  58.6 1.9 %copy-start = (f32[64,1024]{1,0:T(8,128)S(1)}, f32[64,1024]{1,0:T(8,128)}, u32[]{:S(2)}) copy-start(f32[64,1024]{1,0:T(8,128)} %get-tuple-element.5) | copy-start | bytes 786436

commit v3 on v2

--- a/solution.py
+++ b/solution.py
@@ -14,7 +14,7 @@
 PAT = 4
 NBR = 8
 REACH = (-4, -3, -1, 1, 3, 4)
-DOUBLINGS = 9
+DOUBLINGS = 8
 HALF = 64
 
 
@@ -43,11 +43,11 @@
     for mat in mats:
         norm = jnp.max(jnp.sum(jnp.abs(mat), axis=0, keepdims=True), axis=1, keepdims=True)
         scale = 2.0 / (2.0 + norm)
-        start.append((unit - mat * scale, unit * scale, 2.0 * scale))
+        start.append((unit - mat * scale, unit, 2.0 * scale, scale))
 
     def double(_, state):
         new = []
-        for power, series, low in state:
+        for power, series, low, factor in state:
             ph, pl_ = split(power)
             sh, sl = split(series)
             gain = low * (2.0 - low)
@@ -59,12 +59,13 @@
                 square, step = out[:, :B], out[:, B:]
             else:
                 square, step = mm((ph, pl_), (ph, pl_)), mm((ph, pl_), (sh, sl))
-            new.append((square * s + unit * (1.0 - s), (series + step) * s, gain * s))
+            new.append((square * s + unit * (1.0 - s), series + step, gain * s, factor * s))
         return tuple(new)
 
     state = lax.fori_loop(0, DOUBLINGS, double, tuple(start))
     result = []
-    for mat, (_, guess, _) in zip(mats, state):
+    for mat, (_, series, _, factor) in zip(mats, state):
+        guess = series * factor
         gs = split(guess)
         miss = unit - mm(split(mat), gs)
         result.append(guess + mm(gs, split(miss)))
@@ -127,7 +128,7 @@
     return three(nb), three(pos), s
 
 
-def kernel(rows, nbr, slot, tf, cp, res, out_f, out_x, near, yall, uall, x3, acc, tsend, trecv,
+def kernel(rows, nbr, slot, tf, cp, res, out_f, out_x, near, yall, uall, x3, acc, tsend, trecv, dbuf,
            own_sem, x_sem, near_send, near_recv, y_send, y_recv, u_send, u_recv, t_sem, xr_sem):
     r = lax.axis_index("rows")
     g = lax.axis_index("grp")
@@ -201,6 +202,16 @@
         when(there, copy.start)
     for copy in own:
         copy.wait()
+    unit = eye()
+
+    def form(q):
+        total = None
+        for k in range(4):
+            tile = near[q, k]
+            part = dg(tile, tile, 1, 1)
+            total = part if total is None else total + part
+        dbuf[q] = 2.0 * unit + total * (1.0 / B)
+
     middle = (g == 1) | (g == 2)
     first_slab, last_slab = middle & (r == 0), middle & (r == rows - 1)
     for t in range(4):
@@ -208,22 +219,29 @@
         send(inner, near.at[2, t], 0, t, nxt, 4)
         arrived(has_nxt, 7, t)
         send(inner, near.at[7, t], 9, t, prv, 5)
+    form(4)
+    form(5)
     for t in range(4):
         arrived(has_prv, 3, t)
         send(first_slab, near.at[3, t], 1, t, nxt, 8)
         arrived(has_nxt, 6, t)
         send(last_slab, near.at[6, t], 8, t, prv, 9)
+    form(2)
+    form(7)
     for t in range(4):
         arrived(m > 1, 0, t)
         send(has_down, near.at[0, t], 8, t, down, 6)
         arrived(m < count - 2, 9, t)
         send(has_up, near.at[9, t], 1, t, up, 7)
+    for q in (3, 6, 0, 9):
+        form(q)
     for t in range(4):
         arrived(m < count - 2, 8, t)
         arrived(m > 1, 1, t)
+    form(8)
+    form(1)
 
     base = 2 * m - 4
-    unit = eye()
 
     def picks(t):
         return order([nbr[k, t] for k in range(PAT)], NBR * r + t)
@@ -232,12 +250,7 @@
         return jnp.clip(j - base, 0, 9)
 
     def diag(j):
-        total = None
-        for k in range(4):
-            tile = near[place(j), k]
-            part = dg(tile, tile, 1, 1)
-            total = part if total is None else total + part
-        return 2.0 * unit + total * (1.0 / B)
+        return dbuf[place(j)]
 
     def off(x, y):
         scale = jnp.where(linked(x, y), 1.0 / B, 0.0).astype(F32)
@@ -414,6 +427,11 @@
         copy.wait_send()
 
 
+def hand_on(factor, result, out_f, out_x):
+    out_f[...] = factor[...]
+    out_x[...] = result[...]
+
+
 def solution(mesh):
     rows = mesh.shape["rows"]
     smem = pl.BlockSpec(memory_space=pltpu.SMEM)
@@ -439,6 +457,7 @@
                 pltpu.VMEM((16, columns, B), F32),
                 pltpu.VMEM((2, 4, columns, B), BF),
                 pltpu.VMEM((2, 4, columns, B), BF),
+                pltpu.VMEM((10, B, B), F32),
                 dma((4,)), dma((8,)), dma((10, 4)), dma((10, 4)), dma((6, 3)), dma((NBR, 3)),
                 dma((6,)), dma((NBR,)), dma((4,)), dma((4, 4)),
             ],
@@ -446,7 +465,12 @@
                 collective_id=0, has_side_effects=True, vmem_limit_bytes=67043328
             ),
         )(nbr_list.T, setup_slot, tile_factor, coupling, residual)
-        return factor, result
+        return pl.pallas_call(
+            hand_on,
+            out_shape=(jax.ShapeDtypeStruct(factor.shape, F32), jax.ShapeDtypeStruct(result.shape, F32)),
+            in_specs=[whole, whole],
+            out_specs=(whole, whole),
+        )(factor, result)
 
     return jax.shard_map(
         local,

time: 61.3 us -> 59.6 us (0.972)
  local copies, waits for them, and re-layouts: 2.62 us -> 0 us
  Pallas kernels: 57.9 us -> 58.8 us
    unnamed x4 -> x0, local copies, waits for them, and re-layouts: 2.62 us -> none
    pallas_call x0 -> x1, Pallas kernels: none -> 2.02 us  [local(): pl.pallas_call(hand_on, out_shape=(jax.ShapeDtypeStruct(factor.shape, F32...]
    pallas_call x1, Pallas kernels: 57.9 us -> 56.8 us  [local(): pl.pallas_call(functools.partial(kernel, rows), out_shape=(jax.ShapeDtype...]
where the time goes in v3:
time: 59.6 us; the launch traced here: 59.4 us
  Pallas kernels  58.8 us (99%)
  between operations  0.64 us (1%)
    pallas_call x1, Pallas kernels, local(): pl.pallas_call(functools.partial(kernel, rows), out_shape=(jax.ShapeDtype...  56.8 us
    pallas_call x1, Pallas kernels, local(): pl.pallas_call(hand_on, out_shape=(jax.ShapeDtypeStruct(factor.shape, F32...  2.02 us

profile of v3, /device:TPU:6, one launch (start us, length us, event | category | flops | bytes accessed | tf_op | source)
XLA Modules:
  0.0 59.4 jit_solution(4632851354882366745)
XLA Ops:
  0.6 56.8 %shard_map.68 = (f32[2,128,512]{2,1,0:T(8,128)}, f32[64,1024]{1,0:T(8,128)}) custom-call(s32[4,8]{1,0:T(4,128)} %bitcast.1, s32[1,8]{1,0:T(1,128)} %slot.1, bf16[2,128,128]{2,1,0:T(8,128)(2,1)} %tf.1, bf16[2,3,128,128]{3,2,1,0:T(8,128)(2,1)} %cp.1, f32[64,1024]{1,0:T(8,128)} %res.1), custom_call_target="tpu_custom_call" | custom-call | tf_op jit(solution)/shard_map/pallas_call | solution.py:444
  57.4 2.0 %shard_map.69 = (f32[2,128,512]{2,1,0:T(8,128)}, f32[64,1024]{1,0:T(8,128)}) custom-call(f32[2,128,512]{2,1,0:T(8,128)} %get-tuple-element.4.factor, f32[64,1024]{1,0:T(8,128)} %get-tuple-element.5.result), custom_call_target="tpu_custom_call" | custom-call | tf_op jit(solution)/shard_map/pallas_call | solution.py:468

commit v4 on v3

--- a/solution.py
+++ b/solution.py
@@ -75,35 +75,23 @@
 def sweep(mats):
     lane = lax.broadcasted_iota(jnp.int32, (1, B), 1)
     sub = lax.broadcasted_iota(jnp.int32, (8, 1), 0)
-
-    def round_(it, state):
-        done = []
-        for mat in state:
-            mat = list(mat)
-            live = [(it <= p).astype(F32) for p in range(7)]
-            for s in range(7, -1, -1):
-                at = 120 + s
-                row = mat[7][s:s + 1, :]
-                pivot = row[:, at:at + 1]
-                inv = 1.0 / pivot
-                scaled = jnp.where(lane == at, 1.0 + inv, row * inv)
-                for p in range(8):
-                    c = mat[p][:, at:at + 1]
-                    if p == 7:
-                        if s == 0:
-                            continue
-                        c = jnp.where(sub < s, c, 0.0)
-                    else:
-                        c = c * live[p]
-                    mat[p] = mat[p] - c * scaled
-                final = jnp.where((lane >= 8 * it) & (lane < at), 0.0, jnp.where(lane == at, 1.0, row)) * lax.rsqrt(pivot)
-                mat[7] = jnp.where(sub == s, final, mat[7])
-            mat = [pltpu.roll(x, 8, 1) for x in mat]
-            done.append(tuple([mat[7]] + mat[:7]))
-        return tuple(done)
-
-    slabs = lax.fori_loop(0, 8, round_, tuple(tuple(x[8 * p:8 * p + 8, :] for p in range(8)) for x in mats))
-    return [jnp.concatenate(x, axis=0) for x in slabs]
+    work = [[x[8 * p:8 * p + 8, :] for p in range(8)] for x in mats]
+    for k in range(HALF - 1, -1, -1):
+        top, s = divmod(k, 8)
+        at = HALF + k
+        for mat in work:
+            row = mat[top][s:s + 1, :]
+            pivot = row[:, at:at + 1]
+            inv = 1.0 / pivot
+            scaled = jnp.where(lane == at, 1.0 + inv, row * inv)
+            for p in range(top + (s > 0)):
+                c = mat[p][:, at:at + 1]
+                if p == top:
+                    c = jnp.where(sub < s, c, 0.0)
+                mat[p] = mat[p] - c * scaled
+            final = jnp.where(lane < at, 0.0, jnp.where(lane == at, 1.0, row)) * lax.rsqrt(pivot)
+            mat[top] = jnp.where(sub == s, final, mat[top])
+    return [pltpu.roll(jnp.concatenate(x, axis=0), HALF, 1) for x in work]
 
 
 def linked(x, y):

time: 59.6 us -> 57.9 us (0.971)
  Pallas kernels: 58.8 us -> 57 us
    pallas_call x1, Pallas kernels: 56.8 us -> 55 us  [local(): pl.pallas_call(functools.partial(kernel, rows), out_shape=(jax.ShapeDtype...]
where the time goes in v4:
time: 57.9 us; the launch traced here: 57.7 us
  Pallas kernels  57 us (98%)
  between operations  0.64 us (1%)
    pallas_call x1, Pallas kernels, local(): pl.pallas_call(functools.partial(kernel, rows), out_shape=(jax.ShapeDtype...  55 us
    pallas_call x1, Pallas kernels, local(): pl.pallas_call(hand_on, out_shape=(jax.ShapeDtypeStruct(factor.shape, F32...  2.02 us

profile of v4, /device:TPU:6, one launch (start us, length us, event | category | flops | bytes accessed | tf_op | source)
XLA Modules:
  0.0 57.7 jit_solution(12409781773576193550)
XLA Ops:
  0.6 55.0 %shard_map.68 = (f32[2,128,512]{2,1,0:T(8,128)}, f32[64,1024]{1,0:T(8,128)}) custom-call(s32[4,8]{1,0:T(4,128)} %bitcast.1, s32[1,8]{1,0:T(1,128)} %slot.1, bf16[2,128,128]{2,1,0:T(8,128)(2,1)} %tf.1, bf16[2,3,128,128]{3,2,1,0:T(8,128)(2,1)} %cp.1, f32[64,1024]{1,0:T(8,128)} %res.1), custom_call_target="tpu_custom_call" | custom-call | tf_op jit(solution)/shard_map/pallas_call | solution.py:432
  55.7 2.0 %shard_map.69 = (f32[2,128,512]{2,1,0:T(8,128)}, f32[64,1024]{1,0:T(8,128)}) custom-call(f32[2,128,512]{2,1,0:T(8,128)} %get-tuple-element.4.factor, f32[64,1024]{1,0:T(8,128)} %get-tuple-element.5.result), custom_call_target="tpu_custom_call" | custom-call | tf_op jit(solution)/shard_map/pallas_call | solution.py:456

commit v5 on v4

--- a/solution.py
+++ b/solution.py
@@ -186,8 +186,6 @@
     for e in range(4):
         halo.append((has_up, has_down, remote(res.at[:, pl.ds(B * (4 + e), B)], x3.at[e], xr_sem.at[0, e], xr_sem.at[1, e], up)))
         halo.append((has_down, has_up, remote(res.at[:, pl.ds(B * e, B)], x3.at[12 + e], xr_sem.at[2, e], xr_sem.at[3, e], down)))
-    for there, _, copy in halo:
-        when(there, copy.start)
     for copy in own:
         copy.wait()
     unit = eye()
@@ -221,6 +219,8 @@
         send(has_down, near.at[0, t], 8, t, down, 6)
         arrived(m < count - 2, 9, t)
         send(has_up, near.at[9, t], 1, t, up, 7)
+    for there, _, copy in halo:
+        when(there, copy.start)
     for q in (3, 6, 0, 9):
         form(q)
     for t in range(4):

time: 57.9 us -> 57.8 us (level)
  no operation moved by 1% of the time
where the time goes in v5:
time: 57.8 us; the launch traced here: 57.6 us
  Pallas kernels  57 us (99%)
  between operations  0.64 us (1%)
    pallas_call x1, Pallas kernels, local(): pl.pallas_call(functools.partial(kernel, rows), out_shape=(jax.ShapeDtype...  55 us
    pallas_call x1, Pallas kernels, local(): pl.pallas_call(hand_on, out_shape=(jax.ShapeDtypeStruct(factor.shape, F32...  2.02 us

profile of v5, /device:TPU:6, one launch (start us, length us, event | category | flops | bytes accessed | tf_op | source)
XLA Modules:
  0.0 57.6 jit_solution(14301995160551740350)
XLA Ops:
  0.6 55.0 %shard_map.68 = (f32[2,128,512]{2,1,0:T(8,128)}, f32[64,1024]{1,0:T(8,128)}) custom-call(s32[4,8]{1,0:T(4,128)} %bitcast.1, s32[1,8]{1,0:T(1,128)} %slot.1, bf16[2,128,128]{2,1,0:T(8,128)(2,1)} %tf.1, bf16[2,3,128,128]{3,2,1,0:T(8,128)(2,1)} %cp.1, f32[64,1024]{1,0:T(8,128)} %res.1), custom_call_target="tpu_custom_call" | custom-call | tf_op jit(solution)/shard_map/pallas_call | solution.py:432
  55.6 2.0 %shard_map.69 = (f32[2,128,512]{2,1,0:T(8,128)}, f32[64,1024]{1,0:T(8,128)}) custom-call(f32[2,128,512]{2,1,0:T(8,128)} %get-tuple-element.4.factor, f32[64,1024]{1,0:T(8,128)} %get-tuple-element.5.result), custom_call_target="tpu_custom_call" | custom-call | tf_op jit(solution)/shard_map/pallas_call | solution.py:456
